TPU v7x, 32 devices: a whole 2x2x4 slice. The times are simulated.
32 devices in a mesh: freq: 2 (over x), row: 16 (over z, y, core).
Axes of the slice: x: 2, y: 2, z: 4, core: 2. Of those that a mesh axis runs over, the one named last changes fastest.
Arguments:
- data_real: bfloat16 [16384, 8192], P(('freq', 'row')), parts along dimension 0, may hold values from -6 to 6
- data_imag: bfloat16 [16384, 8192], P(('freq', 'row')), parts along dimension 0, may hold values from -6 to 6
- counts: int32 [8, 8], replicated, may hold values from 0 to 4
- source_cols: int32 [128], replicated, may hold values from 0 to 8191, as said below
Outputs:
- pred_real: float32 [16384, 128], P(('freq', 'row')), parts along dimension 0
- pred_imag: float32 [16384, 128], P(('freq', 'row')), parts along dimension 0
There are 2 independent parts, one for each index of `freq`. A program takes and returns all parts, laid end to end along the dimension named above; an argument that names none is the same for every part. Nothing has to cross between parts.
Inputs may be any that keep to these rules, and one draw needn't show every extreme that they name: `source_cols`: 128 distinct grid points; 0 and 8191 are always among them.
All inputs are finite; a program needn't handle non-finite values.
Results may differ from a plain program's by a relative error of at most 0.0029.
Values may be sent and summed in bfloat16 or wider, within the bound.
A program may use at most 128 MiB of HBM per device.

v0:
```python
import math
import jax
import jax.numpy as jnp
from jax import lax
from jax.sharding import PartitionSpec as P

TILES = 8


def tile_weights(counts, row_ids, width):
    tile = width // TILES
    onehot = (row_ids[:, None] // tile == jnp.arange(TILES, dtype=jnp.int32)[None, :]).astype(
        jnp.float32
    )
    table = counts.astype(jnp.float32)
    forward = jnp.dot(onehot, table, precision=lax.Precision.HIGHEST)
    backward = jnp.dot(onehot, table.T, precision=lax.Precision.HIGHEST)
    height = row_ids.shape[0]
    forward = jnp.broadcast_to(forward[:, :, None], (height, TILES, tile)).reshape(height, width)
    backward = jnp.broadcast_to(backward[:, :, None], (height, TILES, tile)).reshape(height, width)
    return (forward, backward)


def complex_pair(left_real, left_imag, right_real, right_imag, dims):
    dot_rr = lax.dot_general(left_real, right_real, dims, preferred_element_type=jnp.float32)
    dot_ii = lax.dot_general(left_imag, right_imag, dims, preferred_element_type=jnp.float32)
    dot_ri = lax.dot_general(left_real, right_imag, dims, preferred_element_type=jnp.float32)
    dot_ir = lax.dot_general(left_imag, right_real, dims, preferred_element_type=jnp.float32)
    return jnp.concatenate([dot_rr - dot_ii, dot_ri + dot_ir], axis=1)


def shards(data_real, data_imag, counts, source_cols):
    rows, width = data_real.shape
    mirror_real, mirror_imag = (
        lax.all_to_all(data_real, "row", split_axis=1, concat_axis=0, tiled=True),
        lax.all_to_all(data_imag, "row", split_axis=1, concat_axis=0, tiled=True),
    )
    row_ids = lax.axis_index("row") * rows + jnp.arange(rows, dtype=jnp.int32)
    forward, backward = tile_weights(counts, row_ids, width)
    denom = jnp.maximum(forward + backward, 1.0)
    sym_real = (
        (forward * data_real.astype(jnp.float32) + backward * mirror_real.T.astype(jnp.float32))
        / denom
    ).astype(jnp.bfloat16)
    sym_imag = (
        (forward * data_imag.astype(jnp.float32) + backward * mirror_imag.T.astype(jnp.float32))
        / denom
    ).astype(jnp.bfloat16)
    panel_real = jnp.take(sym_real, source_cols, axis=1)
    panel_imag = jnp.take(sym_imag, source_cols, axis=1)
    sources = source_cols.shape[0]
    factor = -1.0 / math.sqrt(width)
    piece_real = lax.all_gather(panel_real, "row", axis=0, tiled=True)
    piece_imag = lax.all_gather(panel_imag, "row", axis=0, tiled=True)
    summed = complex_pair(sym_real, sym_imag, piece_real, piece_imag, (((1,), (0,)), ((), ())))
    predicted = factor * summed
    return (predicted[:, :sources], predicted[:, sources:])


def solution(mesh):
    placed = (P(("freq", "row"), None), P(("freq", "row"), None), P(), P())
    return jax.shard_map(
        shards,
        mesh=mesh,
        in_specs=placed,
        out_specs=(P(("freq", "row"), None), P(("freq", "row"), None)),
        check_vma=False,
    )
```

profile of v0, /device:TPU:0, one launch (start us, length us, event | category | flops | bytes accessed | tf_op | source)
XLA Modules:
  0.0 530.0 jit_solution(13418963480100498488)
XLA Ops:
  7.2 7.5 %copy.17 = bf16[64,16,8,512]{3,2,0,1:T(8,128)(2,1)} copy(bf16[64,16,8,512]{3,2,1,0:T(8,128)(2,1)} %bitcast.68) | data formatting | bytes 16777216 | tf_op jit(solution)/shard_map/all_to_all | solution.py:35
  14.7 7.4 %all-to-all-start = ((bf16[512,16,512]{2,0,1:T(8,128)(2,1)}), bf16[512,16,512]{2,0,1:T(8,128)(2,1)}, u32[]{:S(2)}, u32[]{:S(2)}) async-start(bf16[512,16,512]{2,0,1:T(8,128)(2,1)} %bitcast.71), calls=%async_computation | async-start | bytes 16777216 | tf_op jit(solution)/shard_map/all_to_all | solution.py:35
  22.1 7.5 %copy.16 = bf16[64,16,8,512]{3,2,0,1:T(8,128)(2,1)} copy(bf16[64,16,8,512]{3,2,1,0:T(8,128)(2,1)} %bitcast.69) | data formatting | bytes 16777216 | tf_op jit(solution)/shard_map/all_to_all | solution.py:36
  29.7 143.2 %all-to-all-done = bf16[512,16,512]{2,0,1:T(8,128)(2,1)} async-done(((bf16[512,16,512]{2,0,1:T(8,128)(2,1)}), bf16[512,16,512]{2,0,1:T(8,128)(2,1)}, u32[]{:S(2)}, u32[]{:S(2)}) %all-to-all-start) | async-done | bytes 8388640 | tf_op jit(solution)/shard_map/all_to_all | solution.py:35
  172.8 36.5 %all-to-all-start.1 = ((bf16[512,16,512]{2,0,1:T(8,128)(2,1)}), bf16[512,16,512]{2,0,1:T(8,128)(2,1)}, u32[]{:S(2)}, u32[]{:S(2)}) async-start(bf16[512,16,512]{2,0,1:T(8,128)(2,1)} %bitcast.70), calls=%async_computation.1 | async-start | bytes 16777216 | tf_op jit(solution)/shard_map/all_to_all | solution.py:36
  209.4 0.0 all-gather.3.cloned.1.call-start
  209.5 12.0 %copy.6 = bf16[512,8192]{0,1:T(8,128)(2,1)} copy(bf16[512,8192]{1,0:T(8,128)(2,1)} %param.6) | data formatting | bytes 16777216 | tf_op args[0]
  221.4 0.0 copy-start.3
  221.5 0.0 copy-start.2
  221.5 11.5 %copy.8 = bf16[512,8192]{0,1:T(8,128)(2,1)} copy(bf16[512,8192]{1,0:T(8,128)(2,1)} %param.7) | data formatting | bytes 16777216 | tf_op args[1]
  233.0 0.0 copy-done.3
  233.0 0.0 copy-done.2
  233.0 0.3 fusion.7
  233.3 0.3 fusion.8
  233.7 126.5 %all-to-all-done.1 = bf16[512,16,512]{2,0,1:T(8,128)(2,1)} async-done(((bf16[512,16,512]{2,0,1:T(8,128)(2,1)}), bf16[512,16,512]{2,0,1:T(8,128)(2,1)}, u32[]{:S(2)}, u32[]{:S(2)}) %all-to-all-start.1) | async-done | bytes 8388640 | tf_op jit(solution)/shard_map/all_to_all | solution.py:36
  360.1 18.6 %fusion.2 = (bf16[512,8192]{0,1:T(8,128)(2,1)}, bf16[512,8192]{0,1:T(8,128)(2,1)}) fusion(bf16[512,8192]{0,1:T(8,128)(2,1)} %copy.6, f32[512,8]{0,1:T(8,128)S(1)} %fusion.7, f32[512,8]{0,1:T(8,128)S(1)} %fusion.8, bf16[512,16,512]{2,0,1:T(8,128)(2,1)} %all-to-all-done, bf16[512,16,512]{2,0,1:T(8,128)(2,1)} %all-to-all-done.1, bf16[512,8192]{0,1:T(8,128)(2,1)} %copy.8), kind=kLoop, calls=%fused_computation.9 | loop fusion | flops 67108864 | bytes 50364416 | tf_op jit(solution)/shard_map/convert_element_type | solution.py:44
  378.7 5.3 %gather_fusion = bf16[128,512]{1,0:T(8,128)(2,1)S(1)} fusion(bf16[512,8192]{0,1:T(8,128)(2,1)} %get-tuple-element.7, s32[1024]{0:T(1024)S(1)} %pad_clamp_fusion), kind=kCustom, calls=%fused_computation.clone | custom fusion | bytes 262656 | tf_op jit(solution)/shard_map/jit(_take)/gather | solution.py:49
  384.0 5.3 %gather_fusion.1 = bf16[128,512]{1,0:T(8,128)(2,1)S(1)} fusion(bf16[512,8192]{0,1:T(8,128)(2,1)} %get-tuple-element.8, s32[1024]{0:T(1024)S(1)} %pad_clamp_fusion), kind=kCustom, calls=%fused_computation.1.clone | custom fusion | bytes 262656 | tf_op jit(solution)/shard_map/jit(_take)/gather | solution.py:50
  389.3 0.8 select_bitcast_fusion.1
  390.1 0.0 all-gather.3.cloned.1.call-update
  390.2 0.2 all-gather.5.cloned.1.call-start
  390.4 0.5 all-gather.5.cloned.1.call-update
  390.9 72.4 %all-gather.3.cloned.1.call-done = bf16[8192,128]{0,1:T(8,128)(2,1)} async-done(((bf16[512,128]{0,1:T(8,128)(2,1)}), bf16[8192,128]{0,1:T(8,128)(2,1)}) %all-gather.3.cloned.1.call-update) | async-done | bytes 2097168 | tf_op jit(solution)/shard_map/all_gather | solution.py:53
  463.3 5.3 fusion.17
  468.6 37.6 %all-gather.5.cloned.1.call-done = bf16[8192,128]{0,1:T(8,128)(2,1)} async-done(((bf16[512,128]{0,1:T(8,128)(2,1)}), bf16[8192,128]{0,1:T(8,128)(2,1)}) %all-gather.5.cloned.1.call-update) | async-done | bytes 2097168 | tf_op jit(solution)/shard_map/all_gather | solution.py:54
  506.2 0.0 copy-start.1
  506.2 5.4 %fusion.18 = f32[512,128]{0,1:T(8,128)S(1)} fusion(bf16[8192,128]{0,1:T(8,128)(2,1)} %all-gather.5.cloned.1.call-done, bf16[512,8192]{0,1:T(8,128)(2,1)} %get-tuple-element.7), kind=kOutput, calls=%fused_computation.42 | convolution fusion | flops 1073741824 | bytes 10747904 | tf_op jit(solution)/shard_map/dot_general | solution.py:27
  511.6 0.0 copy-done.1
  511.6 0.0 copy-start
  511.6 4.9 convolution_subtract_fusion
  516.6 0.0 copy-done
  516.6 4.8 convolution_add_fusion
  521.3 0.1 maximum_multiply_fusion
  521.5 0.8 copy.10
  522.3 0.8 copy.11
  (5 shorter events, 0.1 us)
Async XLA Ops:
  14.7 158.2 %all-to-all-start = ((bf16[512,16,512]{2,0,1:T(8,128)(2,1)}), bf16[512,16,512]{2,0,1:T(8,128)(2,1)}, u32[]{:S(2)}, u32[]{:S(2)}) async-start(bf16[512,16,512]{2,0,1:T(8,128)(2,1)} %bitcast.71), calls=%async_computation | async-start | bytes 16777216 | tf_op jit(solution)/shard_map/all_to_all | solution.py:35
  172.8 187.3 %all-to-all-start.1 = ((bf16[512,16,512]{2,0,1:T(8,128)(2,1)}), bf16[512,16,512]{2,0,1:T(8,128)(2,1)}, u32[]{:S(2)}, u32[]{:S(2)}) async-start(bf16[512,16,512]{2,0,1:T(8,128)(2,1)} %bitcast.70), calls=%async_computation.1 | async-start | bytes 16777216 | tf_op jit(solution)/shard_map/all_to_all | solution.py:36
  209.4 253.9 %all-gather.3.cloned.1.call-start = ((), (), s32[]{:S(2)}) async-start(), calls=%async_computation.2 | async-start | bytes 2228224 | tf_op jit(solution)/shard_map/all_gather | solution.py:53
  221.4 11.5 %copy-start.3 = (s32[128]{0:T(128)S(1)}, s32[128]{0:T(128)}, u32[]{:S(2)}) copy-start(s32[128]{0:T(128)} %param.9) | copy-start | bytes 1540
  221.5 11.6 %copy-start.2 = (s32[8,8]{1,0:T(8,128)S(1)}, s32[8,8]{1,0:T(8,128)}, u32[]{:S(2)}) copy-start(s32[8,8]{1,0:T(8,128)} %param.8) | copy-start | bytes 772
  390.2 116.0 %all-gather.5.cloned.1.call-start = ((), (), s32[]{:S(2)}) async-start(), calls=%async_computation.3 | async-start | bytes 2228224 | tf_op jit(solution)/shard_map/all_gather | solution.py:54
  506.2 5.4 %copy-start.1 = (bf16[8192,128]{0,1:T(8,128)(2,1)S(1)}, bf16[8192,128]{0,1:T(8,128)(2,1)}, u32[]{:S(2)}) copy-start(bf16[8192,128]{0,1:T(8,128)(2,1)} %all-gather.5.cloned.1.call-done) | copy-start | bytes 6291460
  511.6 4.9 copy-start
Sparse Core Ops, SparseCore 0:
  390.3 72.9 all-gather.2
  466.0 40.1 all-gather.4
where the time goes:
time: 531 us; the launch traced here: 530 us
  waiting for transfers between devices  380 us (72%)
  local copies, waits for them, and re-layouts  50.9 us (10%)
  starting transfers between devices  44.2 us (8%)
  matrix products  21 us (4%)
  other arithmetic  19.4 us (4%)
  between operations  14.2 us (3%)
    all_to_all x1, waiting for transfers between devices, shards(): lax.all_to_all(data_real, 'row', split_axis=1, concat_axis=0, tiled=True)  143 us
    all_to_all x1, waiting for transfers between devices, shards(): lax.all_to_all(data_imag, 'row', split_axis=1, concat_axis=0, tiled=True)  126 us
    all_gather x1, waiting for transfers between devices, shards(): piece_real = lax.all_gather(panel_real, 'row', axis=0, tiled=True)  72.4 us
    all_gather x1, waiting for transfers between devices, shards(): piece_imag = lax.all_gather(panel_imag, 'row', axis=0, tiled=True)  37.6 us
    all_to_all x1, starting transfers between devices, shards(): lax.all_to_all(data_imag, 'row', split_axis=1, concat_axis=0, tiled=True)  36.5 us
    unnamed x12, local copies, waits for them, and re-layouts  25.2 us
    convert_element_type x1, other arithmetic, shards(): sym_real = ((forward * data_real.astype(jnp.float32) + backward * mirror_...  18.6 us
  transfers between devices with their start and end apart: 4, of which 4 were waited for; matrix products, arithmetic and copies ran while one was open for 7% of the time, Pallas kernels for 0%

commit v1 on v0

--- a/solution.py
+++ b/solution.py
@@ -5,6 +5,11 @@
 from jax.sharding import PartitionSpec as P
 
 TILES = 8
+find_hubs = lambda x_in, unit, along_axis: jnp.split(
+    lax.all_gather(jnp.concatenate([x_in, unit], axis=1), axis_name=along_axis, axis=0, tiled=True),
+    [x_in.shape[1]],
+    axis=1,
+)
 
 
 def tile_weights(counts, row_ids, width):
@@ -50,8 +55,7 @@
     panel_imag = jnp.take(sym_imag, source_cols, axis=1)
     sources = source_cols.shape[0]
     factor = -1.0 / math.sqrt(width)
-    piece_real = lax.all_gather(panel_real, "row", axis=0, tiled=True)
-    piece_imag = lax.all_gather(panel_imag, "row", axis=0, tiled=True)
+    piece_real, piece_imag = find_hubs(panel_real, panel_imag, "row")
     summed = complex_pair(sym_real, sym_imag, piece_real, piece_imag, (((1,), (0,)), ((), ())))
     predicted = factor * summed
     return (predicted[:, :sources], predicted[:, sources:])

time: 531 us -> 499 us (0.940)
  waiting for transfers between devices: 380 us -> 355 us
  matrix products: 21 us -> 14.1 us
    all_gather x2 -> x1, waiting for transfers between devices: 110 us -> 85.2 us  [lax.all_gather(jnp.concatenate([x_in, unit], axis=1), axis_name=along_axi...]
    unnamed x12 -> x18, local copies, waits for them, and re-layouts: 25.2 us -> 25.7 us
  transfers between devices with their start and end apart: 4 -> 3, of which waited for: 4 -> 3; matrix products, arithmetic and copies ran while one was open for 7% -> 6% of each run, Pallas kernels for 0% -> 0%
where the time goes in v1:
time: 499 us; the launch traced here: 498 us
  waiting for transfers between devices  355 us (71%)
  local copies, waits for them, and re-layouts  51.5 us (10%)
  starting transfers between devices  44 us (9%)
  other arithmetic  19.4 us (4%)
  between operations  14.2 us (3%)
  matrix products  14.1 us (3%)
    all_to_all x1, waiting for transfers between devices, shards(): lax.all_to_all(data_real, 'row', split_axis=1, concat_axis=0, tiled=True)  143 us
    all_to_all x1, waiting for transfers between devices, shards(): lax.all_to_all(data_imag, 'row', split_axis=1, concat_axis=0, tiled=True)  126 us
    all_gather x1, waiting for transfers between devices, lax.all_gather(jnp.concatenate([x_in, unit], axis=1), axis_name=along_axi...  85.2 us
    all_to_all x1, starting transfers between devices, shards(): lax.all_to_all(data_imag, 'row', split_axis=1, concat_axis=0, tiled=True)  36.5 us
    unnamed x18, local copies, waits for them, and re-layouts  25.7 us
    convert_element_type x1, other arithmetic, shards(): sym_imag = ((forward * data_imag.astype(jnp.float32) + backward * mirror_...  18.6 us
  transfers between devices with their start and end apart: 3, of which 3 were waited for; matrix products, arithmetic and copies ran while one was open for 6% of the time, Pallas kernels for 0%

profile of v1, /device:TPU:0, one launch (start us, length us, event | category | flops | bytes accessed | tf_op | source)
XLA Modules:
  0.0 498.0 jit_solution(15915543845471990008)
XLA Ops:
  7.2 7.5 %copy.17 = bf16[64,16,8,512]{3,2,0,1:T(8,128)(2,1)} copy(bf16[64,16,8,512]{3,2,1,0:T(8,128)(2,1)} %bitcast.68) | data formatting | bytes 16777216 | tf_op jit(solution)/shard_map/all_to_all | solution.py:40
  14.7 7.4 %all-to-all-start = ((bf16[512,16,512]{2,0,1:T(8,128)(2,1)}), bf16[512,16,512]{2,0,1:T(8,128)(2,1)}, u32[]{:S(2)}, u32[]{:S(2)}) async-start(bf16[512,16,512]{2,0,1:T(8,128)(2,1)} %bitcast.71), calls=%async_computation | async-start | bytes 16777216 | tf_op jit(solution)/shard_map/all_to_all | solution.py:40
  22.1 7.5 %copy.16 = bf16[64,16,8,512]{3,2,0,1:T(8,128)(2,1)} copy(bf16[64,16,8,512]{3,2,1,0:T(8,128)(2,1)} %bitcast.69) | data formatting | bytes 16777216 | tf_op jit(solution)/shard_map/all_to_all | solution.py:41
  29.7 143.2 %all-to-all-done = bf16[512,16,512]{2,0,1:T(8,128)(2,1)} async-done(((bf16[512,16,512]{2,0,1:T(8,128)(2,1)}), bf16[512,16,512]{2,0,1:T(8,128)(2,1)}, u32[]{:S(2)}, u32[]{:S(2)}) %all-to-all-start) | async-done | bytes 8388640 | tf_op jit(solution)/shard_map/all_to_all | solution.py:40
  172.8 36.5 %all-to-all-start.1 = ((bf16[512,16,512]{2,0,1:T(8,128)(2,1)}), bf16[512,16,512]{2,0,1:T(8,128)(2,1)}, u32[]{:S(2)}, u32[]{:S(2)}) async-start(bf16[512,16,512]{2,0,1:T(8,128)(2,1)} %bitcast.70), calls=%async_computation.1 | async-start | bytes 16777216 | tf_op jit(solution)/shard_map/all_to_all | solution.py:41
  209.4 0.0 all-gather.2.cloned.1.call-start
  209.4 11.6 %copy.6 = bf16[512,8192]{0,1:T(8,128)(2,1)} copy(bf16[512,8192]{1,0:T(8,128)(2,1)} %param.6) | data formatting | bytes 16777216 | tf_op args[0]
  221.0 0.0 copy-start.2
  221.0 0.0 copy-start.1
  221.0 12.0 %copy.8 = bf16[512,8192]{0,1:T(8,128)(2,1)} copy(bf16[512,8192]{1,0:T(8,128)(2,1)} %param.7) | data formatting | bytes 16777216 | tf_op args[1]
  233.0 0.0 copy-done.2
  233.1 0.0 copy-done.1
  233.1 0.3 fusion.21
  233.4 0.3 fusion.22
  233.7 126.4 %all-to-all-done.1 = bf16[512,16,512]{2,0,1:T(8,128)(2,1)} async-done(((bf16[512,16,512]{2,0,1:T(8,128)(2,1)}), bf16[512,16,512]{2,0,1:T(8,128)(2,1)}, u32[]{:S(2)}, u32[]{:S(2)}) %all-to-all-start.1) | async-done | bytes 8388640 | tf_op jit(solution)/shard_map/all_to_all | solution.py:41
  360.1 18.6 %fusion.5 = (bf16[512,8192]{0,1:T(8,128)(2,1)}, bf16[512,8192]{0,1:T(8,128)(2,1)}) fusion(bf16[512,8192]{0,1:T(8,128)(2,1)} %copy.8, f32[512,8]{0,1:T(8,128)S(1)} %fusion.21, f32[512,8]{0,1:T(8,128)S(1)} %fusion.22, bf16[512,16,512]{2,0,1:T(8,128)(2,1)} %all-to-all-done.1, bf16[512,16,512]{2,0,1:T(8,128)(2,1)} %all-to-all-done, bf16[512,8192]{0,1:T(8,128)(2,1)} %copy.6), kind=kLoop, calls=%fused_computation.12 | loop fusion | flops 67108864 | bytes 50364416 | tf_op jit(solution)/shard_map/convert_element_type | solution.py:53
  378.6 5.3 %gather_fusion = bf16[128,512]{1,0:T(8,128)(2,1)S(1)} fusion(bf16[512,8192]{0,1:T(8,128)(2,1)} %get-tuple-element.8, s32[1024]{0:T(1024)S(1)} %pad_clamp_fusion), kind=kCustom, calls=%fused_computation.clone | custom fusion | bytes 262656 | tf_op jit(solution)/shard_map/jit(_take)/gather | solution.py:54
  384.0 5.3 %gather_fusion.1 = bf16[128,512]{1,0:T(8,128)(2,1)S(1)} fusion(bf16[512,8192]{0,1:T(8,128)(2,1)} %get-tuple-element.7, s32[1024]{0:T(1024)S(1)} %pad_clamp_fusion), kind=kCustom, calls=%fused_computation.1.clone | custom fusion | bytes 262656 | tf_op jit(solution)/shard_map/jit(_take)/gather | solution.py:55
  389.3 0.1 select_bitcast_fusion.1
  389.4 0.7 pad_maximum_fusion
  390.1 0.0 all-gather.2.cloned.1.call-update
  390.2 85.2 %all-gather.2.cloned.1.call-done = bf16[8192,256]{0,1:T(8,128)(2,1)} async-done(((bf16[512,256]{0,1:T(8,128)(2,1)}), bf16[8192,256]{0,1:T(8,128)(2,1)}) %all-gather.2.cloned.1.call-update) | async-done | bytes 4194320 | tf_op jit(solution)/shard_map/all_gather | solution.py:9
  475.3 0.0 copy-start
  475.3 0.0 slice-start.2
  475.3 0.0 slice-start
  475.4 5.4 %fusion.7 = f32[512,128]{0,1:T(8,128)S(1)} fusion(bf16[512,8192]{0,1:T(8,128)(2,1)} %get-tuple-element.7, bf16[8192,256]{0,1:T(8,128)(2,1)} %all-gather.2.cloned.1.call-done), kind=kOutput, calls=%fused_computation.16 | convolution fusion | flops 1073741824 | bytes 10747904 | tf_op jit(solution)/shard_map/dot_general | solution.py:31
  480.8 0.0 copy-done
  480.8 0.0 slice-start.3
  480.8 0.0 slice-start.1
  480.8 5.6 %fusion.9 = f32[512,128]{0,1:T(8,128)S(1)} fusion(bf16[512,8192]{0,1:T(8,128)(2,1)} %get-tuple-element.8, bf16[8192,256]{0,1:T(8,128)(2,1)S(1)} %copy-done), kind=kOutput, calls=%fused_computation.18 | convolution fusion | flops 1073741824 | bytes 10747904 | tf_op jit(solution)/shard_map/dot_general | solution.py:32
  486.4 0.0 slice-done.2
  486.4 0.4 slice-done.3
  486.8 1.3 fusion.18
  488.1 0.0 slice-done
  488.1 0.0 slice-done.1
  488.1 1.3 fusion.15
  489.4 0.1 maximum_multiply_fusion
  489.5 0.8 copy.10
  490.3 0.8 copy.11
  (7 shorter events, 0.1 us)
Async XLA Ops:
  14.7 158.2 %all-to-all-start = ((bf16[512,16,512]{2,0,1:T(8,128)(2,1)}), bf16[512,16,512]{2,0,1:T(8,128)(2,1)}, u32[]{:S(2)}, u32[]{:S(2)}) async-start(bf16[512,16,512]{2,0,1:T(8,128)(2,1)} %bitcast.71), calls=%async_computation | async-start | bytes 16777216 | tf_op jit(solution)/shard_map/all_to_all | solution.py:40
  172.8 187.3 %all-to-all-start.1 = ((bf16[512,16,512]{2,0,1:T(8,128)(2,1)}), bf16[512,16,512]{2,0,1:T(8,128)(2,1)}, u32[]{:S(2)}, u32[]{:S(2)}) async-start(bf16[512,16,512]{2,0,1:T(8,128)(2,1)} %bitcast.70), calls=%async_computation.1 | async-start | bytes 16777216 | tf_op jit(solution)/shard_map/all_to_all | solution.py:41
  209.4 266.0 %all-gather.2.cloned.1.call-start = ((), (), s32[]{:S(2)}) async-start(), calls=%async_computation.2 | async-start | bytes 4456448 | tf_op jit(solution)/shard_map/all_gather | solution.py:9
  221.0 12.0 %copy-start.2 = (s32[128]{0:T(128)S(1)}, s32[128]{0:T(128)}, u32[]{:S(2)}) copy-start(s32[128]{0:T(128)} %param.9) | copy-start | bytes 1540
  221.0 12.1 %copy-start.1 = (s32[8,8]{1,0:T(8,128)S(1)}, s32[8,8]{1,0:T(8,128)}, u32[]{:S(2)}) copy-start(s32[8,8]{1,0:T(8,128)} %param.8) | copy-start | bytes 772
  475.3 5.4 %copy-start = (bf16[8192,256]{0,1:T(8,128)(2,1)S(1)}, bf16[8192,256]{0,1:T(8,128)(2,1)}, u32[]{:S(2)}) copy-start(bf16[8192,256]{0,1:T(8,128)(2,1)} %all-gather.2.cloned.1.call-done) | copy-start | bytes 12582916
  475.3 11.0 %slice-start.2 = ((s8[8388608]{0:T(1024)(128)(4,1)}), s8[4194304]{0:T(1024)(128)(4,1)S(1)}, s32[]{:S(2)}) async-start(s8[8388608]{0:T(1024)(128)(4,1)} %bitcast.66), calls=%async_computation.5 | async-start | bytes 8388608
  475.3 12.7 %slice-start = ((s8[8388608]{0:T(1024)(128)(4,1)}), s8[4194304]{0:T(1024)(128)(4,1)S(1)}, s32[]{:S(2)}) async-start(s8[8388608]{0:T(1024)(128)(4,1)} %bitcast.64), calls=%async_computation.3 | async-start | bytes 8388608
  480.8 6.0 %slice-start.3 = ((s8[8388608]{0:T(1024)(128)(4,1)}), s8[4194304]{0:T(1024)(128)(4,1)S(1)}, s32[]{:S(2)}) async-start(s8[8388608]{0:T(1024)(128)(4,1)} %bitcast.66), calls=%async_computation.6 | async-start | bytes 8388608
  480.8 7.3 %slice-start.1 = ((s8[8388608]{0:T(1024)(128)(4,1)}), s8[4194304]{0:T(1024)(128)(4,1)S(1)}, s32[]{:S(2)}) async-start(s8[8388608]{0:T(1024)(128)(4,1)} %bitcast.64), calls=%async_computation.4 | async-start | bytes 8388608
Sparse Core Ops, SparseCore 0:
  390.3 85.0 all-gather.1
